TPU v7x, 32 devices: a whole 2x2x4 slice. The times are simulated.
32 devices in a mesh: blocks: 2 (over y), rows: 4 (over z), cols: 4 (over x, core).
Axes of the slice: x: 2, y: 2, z: 4, core: 2. Of those that a mesh axis runs over, the one named last changes fastest.
Arguments:
- sens_tiles: bfloat16 [128, 1024, 256], P(('blocks', 'rows'), 'cols'), parts along dimension 0, may hold values from -10.606602 to 10.606602, as said below
- tile_coords: int32 [128, 8], P(('blocks', 'rows'), 'cols'), parts along dimension 0, may hold values from 0 to 7, as said below
- tile_counts: int32 [8, 4], P(('blocks', 'rows'), 'cols'), parts along dimension 0, may hold values from 3 to 16, as said below
- data_vec: float32 [192, 4096], P('blocks', 'rows'), parts along dimension 0, may hold values from -6 to 6
- cell_vec: float32 [192, 8192], P('blocks', 'cols'), parts along dimension 0, may hold values from -6 to 6
- alpha_now: float32 [192], P('blocks'), parts along dimension 0, may hold values from 0.5 to 2
Outputs:
- data_next: float32 [192, 4096], P('blocks', 'rows'), parts along dimension 0
- cell_next: float32 [192, 8192], P('blocks', 'cols'), parts along dimension 0
- beta_next: float32 [192], P('blocks'), parts along dimension 0
- alpha_next: float32 [192], P('blocks'), parts along dimension 0
There are 2 independent parts, one for each index of `blocks`. A program takes and returns all parts, laid end to end along the dimension named above; each array names one. Nothing has to cross between parts.
Inputs may be any that keep to these rules, and one draw needn't show every extreme that they name: `sens_tiles`: entries of the tiles; slots at or beyond a device's count hold values that belong to no tile. `tile_coords`: within one device all 16 slots name distinct (row tile, column tile) pairs; the first entry of a pair is below 4, the second below 8. `tile_counts`: every data-row band has one device whose count is 16.
All inputs are finite; a program needn't handle non-finite values.
Results may differ from a plain program's by a relative error of at most 0.0043.
Values sent between devices are 32-bit elements; how exact they have to be, the bound alone decides.
No kernel may reach another device: no remote copies, remote signals or barrier semaphores. Data moves between devices by JAX's collectives and lax.ppermute only.
A program may use at most 64 MiB of HBM per device.

v0:
```python
import jax
import jax.numpy as jnp
from jax import lax
from jax.sharding import PartitionSpec as P

EPSILON = 1e-06


def listed_mask(sens_tiles, listed_count):
    return (jnp.arange(sens_tiles.shape[0], dtype=jnp.int32) < listed_count).astype(jnp.float32)


def forward_sweep(sens_tiles, tile_coords, listed_count, cell_low, row_tiles):
    samples = cell_low.shape[0]
    tile_size = sens_tiles.shape[1]
    listed = listed_mask(sens_tiles, listed_count)
    blocks = cell_low.reshape(samples, cell_low.shape[1] // tile_size, tile_size)
    picked = jnp.take(blocks, tile_coords[:, 1], axis=1)
    contrib = jnp.einsum("ktj,tij->kti", picked, sens_tiles, preferred_element_type=jnp.float32)
    spread = jax.nn.one_hot(tile_coords[:, 0], row_tiles, dtype=jnp.float32) * listed[:, None]
    placed = jnp.einsum("kti,tr->kri", contrib, spread, precision=lax.Precision.HIGHEST)
    return placed.reshape(samples, row_tiles * tile_size)


def adjoint_sweep(sens_tiles, tile_coords, listed_count, data_low, col_tiles):
    samples = data_low.shape[0]
    tile_size = sens_tiles.shape[1]
    listed = listed_mask(sens_tiles, listed_count)
    blocks = data_low.reshape(samples, data_low.shape[1] // tile_size, tile_size)
    picked = jnp.take(blocks, tile_coords[:, 0], axis=1)
    contrib = jnp.einsum("kti,tij->ktj", picked, sens_tiles, preferred_element_type=jnp.float32)
    spread = jax.nn.one_hot(tile_coords[:, 1], col_tiles, dtype=jnp.float32) * listed[:, None]
    placed = jnp.einsum("ktj,ts->ksj", contrib, spread, precision=lax.Precision.HIGHEST)
    return placed.reshape(samples, col_tiles * tile_size)


def per_device(sens_tiles, tile_coords, tile_counts, data_vec, cell_vec, alpha_now):
    tile_size = sens_tiles.shape[1]
    row_tiles = data_vec.shape[1] // tile_size
    col_tiles = cell_vec.shape[1] // tile_size
    listed_count = tile_counts[0, 0]
    data_total = data_vec.shape[1] * lax.axis_size("rows")
    cell_total = cell_vec.shape[1] * lax.axis_size("cols")
    cell_low = cell_vec.astype(jnp.bfloat16)
    partial_rows = forward_sweep(sens_tiles, tile_coords, listed_count, cell_low, row_tiles)
    row_full = lax.psum(partial_rows, "cols")
    residual = row_full - alpha_now[:, None] * data_vec
    squares = lax.psum(jnp.sum(residual * residual, axis=1), "rows")
    beta_next = jnp.sqrt(squares / data_total + EPSILON)
    data_next = residual / beta_next[:, None]
    data_low = data_next.astype(jnp.bfloat16)
    partial_cells = adjoint_sweep(sens_tiles, tile_coords, listed_count, data_low, col_tiles)
    cell_full = lax.psum(partial_cells, "rows")
    fresh = cell_full - beta_next[:, None] * cell_vec
    sumsq = lax.psum(jnp.sum(fresh * fresh, axis=1), "cols")
    alpha_next = jnp.sqrt(sumsq / cell_total + EPSILON)
    cell_next = fresh / alpha_next[:, None]
    return (data_next, cell_next, beta_next, alpha_next)


def solution(mesh):
    placed = (
        P(("blocks", "rows"), "cols", None),
        P(("blocks", "rows"), "cols"),
        P(("blocks", "rows"), "cols"),
        P("blocks", "rows"),
        P("blocks", "cols"),
        P("blocks"),
    )
    return jax.shard_map(
        per_device,
        mesh=mesh,
        in_specs=placed,
        out_specs=(P("blocks", "rows"), P("blocks", "cols"), P("blocks"), P("blocks")),
        check_vma=False,
    )
```

profile of v0, /device:TPU:0, one launch (start us, length us, event | category | flops | bytes accessed | tf_op | source)
XLA Modules:
  0.0 127.0 jit_solution(8777433551403314318)
XLA Ops:
  7.2 0.0 copy-start
  7.2 0.0 all-reduce.3.cloned.1.call-start
  7.2 0.8 and_bitcast_fusion
  8.1 0.8 slice_bitcast_fusion
  9.5 1.2 convert_element_type.19
  10.7 0.6 gather_fusion
  11.3 0.0 copy-done
  11.3 0.8 convolution_bitcast_fusion.1
  12.1 0.0 copy-start.2
  12.1 0.0 copy-start.4
  12.1 1.7 %fusion.2 = f32[4,96,256]{2,0,1:T(4,128)S(1)} fusion(f32[96,16,256]{2,0,1:T(8,128)S(1)} %convolution_bitcast_fusion.1, f32[16]{0:T(128)S(1)} %compare_convert_fusion, s32[16]{0:T(128)S(1)} %get-tuple-element.9), kind=kOutput, calls=%fused_computation.4 | convolution fusion | flops 18874496 | bytes 1966208 | tf_op jit(solution)/shard_map/kti,tr->kri/dot_general | solution.py:21
  13.9 0.8 copy.16
  14.7 0.0 all-reduce.3.cloned.1.call-update
  14.7 0.0 all-reduce.5.cloned.1.call-start
  14.8 35.6 %all-reduce.3.cloned.1.call-done = f32[96,1024]{1,0:T(8,128)} async-done(((f32[96,1024]{1,0:T(8,128)}), f32[96,1024]{1,0:T(8,128)}) %all-reduce.3.cloned.1.call-update) | async-done | bytes 393232 | tf_op jit(solution)/shard_map/psum | solution.py:46
  50.4 0.0 copy-done.2
  50.4 0.0 copy-done.4
  50.4 1.2 multiply_reduce_fusion.1
  51.6 11.7 %psum.29 = f32[96]{0:T(128)S(1)} all-reduce(f32[96]{0:T(128)S(1)} %multiply_reduce_fusion.1), channel_id=1, replica_groups=mesh['blocks'=2,'rows'=4,'cols'=4] {'rows'}, use_global_device_ids=true, to_apply=%region_2.3 | all-reduce | flops 96 | bytes 768 | tf_op jit(solution)/shard_map/psum | solution.py:48
  63.3 0.0 copy-start.3
  63.3 1.9 %fusion.28 = (bf16[96,1024]{1,0:T(8,128)(2,1)S(1)}, f32[96,1024]{1,0:T(8,128)}) fusion(f32[96]{0:T(128)S(1)} %add_sqrt_fusion.1, f32[96,1024]{1,0:T(8,128)} %all-reduce.3.cloned.1.call-done, f32[96,1024]{1,0:T(8,128)S(1)} %copy-done.2, f32[96]{0:T(128)S(1)} %copy-done.4), kind=kLoop, calls=%fused_computation.53 | loop fusion | flops 393216 | bytes 1377024 | tf_op jit(solution)/shard_map/convert_element_type | solution.py:51
  65.2 0.6 gather_fusion.1
  65.8 0.5 convolution_bitcast_fusion
  66.3 1.7 %fusion = f32[8,96,256]{2,0,1:T(8,128)S(1)} fusion(f32[96,16,256]{2,0,1:T(8,128)S(1)} %convolution_bitcast_fusion, f32[16]{0:T(128)S(1)} %compare_convert_fusion, s32[16]{0:T(128)S(1)} %get-tuple-element.6), kind=kOutput, calls=%fused_computation.2 | convolution fusion | flops 37748992 | bytes 2359424 | tf_op jit(solution)/shard_map/ktj,ts->ksj/dot_general | solution.py:33
  68.1 0.0 copy-start.1
  68.1 1.1 copy.17
  69.2 0.0 all-reduce.5.cloned.1.call-update
  69.2 41.3 %all-reduce.5.cloned.1.call-done = f32[96,2048]{1,0:T(8,128)} async-done(((f32[96,2048]{1,0:T(8,128)}), f32[96,2048]{1,0:T(8,128)}) %all-reduce.5.cloned.1.call-update) | async-done | bytes 786448 | tf_op jit(solution)/shard_map/psum | solution.py:53
  110.5 0.0 copy-done.1
  110.5 1.4 %multiply_reduce_fusion = f32[96]{0:T(128)S(1)} fusion(f32[96,2048]{1,0:T(8,128)} %all-reduce.5.cloned.1.call-done, f32[96,2048]{1,0:T(8,128)S(1)} %copy-done.1, f32[96]{0:T(128)S(1)} %add_sqrt_fusion.1), kind=kLoop, calls=%fused_computation.12 | loop fusion | flops 786336 | bytes 1573632 | tf_op jit(solution)/shard_map/reduce_sum | solution.py:55
  111.9 6.0 %psum.31 = f32[96]{0:T(128)S(1)} all-reduce(f32[96]{0:T(128)S(1)} %multiply_reduce_fusion), channel_id=1, replica_groups=mesh['blocks'=2,'rows'=4,'cols'=4] {'cols'}, use_global_device_ids=true, to_apply=%region_5.6 | all-reduce | flops 96 | bytes 768 | tf_op jit(solution)/shard_map/psum | solution.py:55
  118.0 0.0 copy-done.3
  118.0 0.0 copy-start.5
  118.0 2.2 %broadcast_divide_fusion = f32[96,2048]{1,0:T(8,128)} fusion(f32[96]{0:T(128)S(1)} %add_sqrt_fusion, f32[96,2048]{1,0:T(8,128)} %all-reduce.5.cloned.1.call-done, f32[96,2048]{1,0:T(8,128)S(1)} %copy-done.1, f32[96]{0:T(128)S(1)} %add_sqrt_fusion.1), kind=kLoop, calls=%fused_computation.19 | loop fusion | flops 589824 | bytes 2360064 | tf_op jit(solution)/shard_map/div | solution.py:57
  120.2 0.0 copy-done.5
  (6 shorter events, 0.1 us)
Async XLA Ops:
  7.2 4.2 %copy-start = (bf16[16,256,256]{2,1,0:T(8,128)(2,1)S(1)}, bf16[16,256,256]{2,1,0:T(8,128)(2,1)}, u32[]{:S(2)}) copy-start(bf16[16,256,256]{2,1,0:T(8,128)(2,1)} %param.6) | copy-start | bytes 6291460
  7.2 43.2 %all-reduce.3.cloned.1.call-start = ((), (), s32[]{:S(2)}) async-start(), calls=%async_computation | async-start | bytes 786432 | tf_op jit(solution)/shard_map/psum | solution.py:46
  12.1 38.3 %copy-start.2 = (f32[96,1024]{1,0:T(8,128)S(1)}, f32[96,1024]{1,0:T(8,128)}, u32[]{:S(2)}) copy-start(f32[96,1024]{1,0:T(8,128)} %param.9) | copy-start | bytes 1179652
  12.1 38.3 %copy-start.4 = (f32[96]{0:T(128)S(1)}, f32[96]{0:T(128)}, u32[]{:S(2)}) copy-start(f32[96]{0:T(128)} %param.11) | copy-start | bytes 1156
  14.7 95.8 %all-reduce.5.cloned.1.call-start = ((), (), s32[]{:S(2)}) async-start(), calls=%async_computation.1 | async-start | bytes 1572864 | tf_op jit(solution)/shard_map/psum | solution.py:53
  63.3 54.7 %copy-start.3 = (f32[96]{0:T(128)}, f32[96]{0:T(128)S(1)}, u32[]{:S(2)}) copy-start(f32[96]{0:T(128)S(1)} %add_sqrt_fusion.1) | copy-start | bytes 1156
  68.1 42.5 %copy-start.1 = (f32[96,2048]{1,0:T(8,128)S(1)}, f32[96,2048]{1,0:T(8,128)}, u32[]{:S(2)}) copy-start(f32[96,2048]{1,0:T(8,128)} %param.10) | copy-start | bytes 2359300
  118.0 2.2 %copy-start.5 = (f32[96]{0:T(128)}, f32[96]{0:T(128)S(1)}, u32[]{:S(2)}) copy-start(f32[96]{0:T(128)S(1)} %add_sqrt_fusion) | copy-start | bytes 1156
Sparse Core Ops, SparseCore 0:
  14.8 35.5 all-reduce.2
  69.3 41.1 all-reduce.4
where the time goes:
time: 127 us
  waiting for transfers between devices  77 us (61%)
  blocking collectives  17.7 us (14%)
  between operations  14.8 us (12%)
  other arithmetic  9.5 us (7%)
  matrix products  4.7 us (4%)
  local copies, waits for them, and re-layouts  3.22 us (3%)
    psum x1, waiting for transfers between devices, per_device(): cell_full = lax.psum(partial_cells, 'rows')  41.3 us
    psum x1, waiting for transfers between devices, per_device(): row_full = lax.psum(partial_rows, 'cols')  35.6 us
    psum x1, blocking collectives, per_device(): squares = lax.psum(jnp.sum(residual * residual, axis=1), 'rows')  11.7 us
    psum x1, blocking collectives, per_device(): sumsq = lax.psum(jnp.sum(fresh * fresh, axis=1), 'cols')  6.04 us
  transfers between devices with their start and end apart: 2, of which 2 were waited for; matrix products, arithmetic and copies ran while one was open for 0% of the time, Pallas kernels for 0%

commit v1 on v0

v1 whole, which is shorter than its diff:
```python
import functools

import jax
import jax.numpy as jnp
from jax import lax
from jax.experimental import pallas as pl
from jax.experimental.pallas import tpu as pltpu
from jax.sharding import PartitionSpec as P

EPSILON = 1e-06
LANES = 128
CHUNKS = 4
GRANT = pltpu.CompilerParams(vmem_limit_bytes=12 << 20)

F32 = jnp.float32
BF16 = jnp.bfloat16
NT = (((1,), (1,)), ((), ()))
NN = (((1,), (0,)), ((), ()))


def vmem():
    return pl.BlockSpec(memory_space=pltpu.VMEM)


def smem():
    return pl.BlockSpec(memory_space=pltpu.SMEM)


def diagonal(samples):
    rows = lax.broadcasted_iota(jnp.int32, (samples, LANES), 0)
    lanes = lax.broadcasted_iota(jnp.int32, (samples, LANES), 1)
    return rows == lanes


def as_row(column):
    picked = jnp.where(diagonal(column.shape[0]), column, 0.0)
    return jnp.sum(picked, axis=0, keepdims=True)


def as_column(row, samples):
    picked = jnp.where(diagonal(samples), row, 0.0)
    return jnp.sum(picked, axis=1, keepdims=True)


def forward_kernel(coords, count, cell_ref, tiles_ref, *rest):
    outs, cells, acc = rest[:-2], rest[-2], rest[-1]
    slots, tile = tiles_ref.shape[:2]
    part_samples = outs[0].shape[0]
    for c in range(cells.shape[0]):
        cells[c] = cell_ref[:, c * tile : (c + 1) * tile].astype(BF16)
    acc[...] = jnp.zeros_like(acc)
    for t in range(slots):
        part = lax.dot_general(cells[coords[t, 1]], tiles_ref[t], NT, preferred_element_type=F32)
        acc[coords[t, 0]] += jnp.where(t < count[0, 0], part, 0.0)
    for m, out in enumerate(outs):
        for r in range(acc.shape[0]):
            out[:, r * tile : (r + 1) * tile] = acc[r, m * part_samples : (m + 1) * part_samples]


def forward(coords, count, cell_vec, tiles, row_tiles, chunks):
    samples, cells = cell_vec.shape
    tile = tiles.shape[1]
    return pl.pallas_call(
        forward_kernel,
        out_shape=[jax.ShapeDtypeStruct((samples // chunks, row_tiles * tile), F32)] * chunks,
        in_specs=[smem(), smem(), vmem(), vmem()],
        out_specs=[vmem()] * chunks,
        scratch_shapes=[
            pltpu.VMEM((cells // tile, samples, tile), BF16),
            pltpu.VMEM((row_tiles, samples, tile), F32),
        ],
        compiler_params=GRANT,
        name="forward",
    )(coords, count, cell_vec, tiles)


def backward_kernel(m, coords, count, half, ours, theirs, data_ref, alpha_ref, tiles_ref, keep, send, residual, squares, low, acc):
    slots, tile = tiles_ref.shape[:2]
    samples = ours.shape[0]
    rows = slice(m * samples, (m + 1) * samples)
    value = ours[...] + theirs[...] - alpha_ref[rows] * data_ref[rows]
    residual[...] = value
    squares[...] = as_row(jnp.sum(value * value, axis=1, keepdims=True))
    for r in range(low.shape[0]):
        low[r] = value[:, r * tile : (r + 1) * tile].astype(BF16)
    acc[...] = jnp.zeros_like(acc)
    for t in range(slots):
        part = lax.dot_general(low[coords[t, 0]], tiles_ref[t], NN, preferred_element_type=F32)
        acc[coords[t, 1]] += jnp.where(t < count[0, 0], part, 0.0)
    width = acc.shape[0] // 2
    for c in range(width):
        keep[:, c * tile : (c + 1) * tile] = acc[half[0] * width + c]
        send[:, c * tile : (c + 1) * tile] = acc[(1 - half[0]) * width + c]


def backward(m, coords, count, half, ours, theirs, data_vec, alpha, tiles, col_tiles):
    samples, data = ours.shape
    tile = tiles.shape[1]
    piece = jax.ShapeDtypeStruct((samples, col_tiles * tile // 2), F32)
    return pl.pallas_call(
        functools.partial(backward_kernel, m),
        out_shape=[
            piece,
            piece,
            jax.ShapeDtypeStruct((samples, data), F32),
            jax.ShapeDtypeStruct((1, LANES), F32),
        ],
        in_specs=[smem()] * 3 + [vmem()] * 5,
        out_specs=[vmem()] * 4,
        scratch_shapes=[
            pltpu.VMEM((data // tile, samples, tile), BF16),
            pltpu.VMEM((col_tiles, samples, tile), F32),
        ],
        compiler_params=GRANT,
        name=f"backward_{m}",
    )(coords, count, half, ours, theirs, data_vec, alpha, tiles)


def fresh_kernel(m, total, half, ours, theirs, sums, cell_ref, fresh, squares):
    samples, width = ours.shape
    beta = jnp.sqrt(as_column(sums[m : m + 1], samples) / total + EPSILON)
    cells = cell_ref[m * samples : (m + 1) * samples, pl.ds(pl.multiple_of(half[0] * width, LANES), width)]
    value = (ours[...] + theirs[...]) / beta - beta * cells
    fresh[...] = value
    squares[...] = as_row(jnp.sum(value * value, axis=1, keepdims=True))


def fresh_piece(m, total, half, ours, theirs, sums, cell_vec):
    return pl.pallas_call(
        functools.partial(fresh_kernel, m, total),
        out_shape=[jax.ShapeDtypeStruct(ours.shape, F32), jax.ShapeDtypeStruct((1, LANES), F32)],
        in_specs=[smem()] + [vmem()] * 4,
        out_specs=[vmem()] * 2,
        compiler_params=GRANT,
        name=f"fresh_{m}",
    )(half, ours, theirs, sums, cell_vec)


def data_kernel(total, sums, *rest):
    chunks = sums.shape[0]
    residuals, out, beta_row = rest[:chunks], rest[chunks], rest[chunks + 1]
    samples = residuals[0].shape[0]
    beta_row[...] = jnp.sqrt(sums[...] / total + EPSILON)
    for m in range(chunks):
        beta = jnp.sqrt(as_column(sums[m : m + 1], samples) / total + EPSILON)
        out[m * samples : (m + 1) * samples] = residuals[m][...] / beta


def data_out(total, sums, residuals):
    samples, data = residuals[0].shape
    return pl.pallas_call(
        functools.partial(data_kernel, total),
        out_shape=[
            jax.ShapeDtypeStruct((samples * len(residuals), data), F32),
            jax.ShapeDtypeStruct(sums.shape, F32),
        ],
        in_specs=[vmem()] * (1 + len(residuals)),
        out_specs=[vmem()] * 2,
        compiler_params=GRANT,
        name="data_out",
    )(sums, *residuals)


def cell_kernel(total, half, sums, *rest):
    chunks = sums.shape[0]
    ours, theirs = rest[:chunks], rest[chunks : 2 * chunks]
    out, alpha_row = rest[2 * chunks :]
    samples, width = ours[0].shape
    alpha_row[...] = jnp.sqrt(sums[...] / total + EPSILON)
    for m in range(chunks):
        rows = slice(m * samples, (m + 1) * samples)
        scale = 1.0 / jnp.sqrt(as_column(sums[m : m + 1], samples) / total + EPSILON)
        out[rows, pl.ds(pl.multiple_of(half[0] * width, LANES), width)] = ours[m][...] * scale
        out[rows, pl.ds(pl.multiple_of((1 - half[0]) * width, LANES), width)] = theirs[m][...] * scale


def cell_out(total, half, sums, ours, theirs):
    samples, width = ours[0].shape
    return pl.pallas_call(
        functools.partial(cell_kernel, total),
        out_shape=[
            jax.ShapeDtypeStruct((samples * len(ours), 2 * width), F32),
            jax.ShapeDtypeStruct(sums.shape, F32),
        ],
        in_specs=[smem(), vmem()] + [vmem()] * (2 * len(ours)),
        out_specs=[vmem()] * 2,
        compiler_params=GRANT,
        name="cell_out",
    )(half, sums, *ours, *theirs)


def bits_of(axis):
    size = lax.axis_size(axis)
    if size < 2 or size & (size - 1):
        raise ValueError("axis size")
    return [1 << b for b in range(size.bit_length() - 1)]


def swap(value, axis, bit):
    return lax.ppermute(value, axis, [(i, i ^ bit) for i in range(lax.axis_size(axis))])


def add_up(value, axis, bits):
    for bit in bits:
        value = value + swap(value, axis, bit)
    return value


def spread_rows(rows, samples):
    return rows[:, :samples].reshape(-1)


def per_device(sens_tiles, tile_coords, tile_counts, data_vec, cell_vec, alpha_now):
    tile = sens_tiles.shape[1]
    samples = data_vec.shape[0]
    row_tiles = data_vec.shape[1] // tile
    col_tiles = cell_vec.shape[1] // tile
    chunks = CHUNKS
    part = samples // chunks
    data_total = data_vec.shape[1] * lax.axis_size("rows")
    cell_total = cell_vec.shape[1] * lax.axis_size("cols")
    row_bits, col_bits = bits_of("rows"), bits_of("cols")
    half = (lax.axis_index("rows") % 2).astype(jnp.int32).reshape(1)
    alpha = alpha_now[:, None]

    partial = forward(tile_coords, tile_counts, cell_vec, sens_tiles, row_tiles, chunks)
    ours = [add_up(p, "cols", col_bits[:0:-1]) for p in partial]
    theirs = [swap(p, "cols", col_bits[0]) for p in ours]
    keeps, sends, residuals, squares = zip(
        *[
            backward(m, tile_coords, tile_counts, half, ours[m], theirs[m], data_vec, alpha, sens_tiles, col_tiles)
            for m in range(chunks)
        ]
    )
    pieces = [keep + swap(send, "rows", row_bits[0]) for keep, send in zip(keeps, sends)]
    data_sums = add_up(jnp.concatenate(squares, 0), "rows", row_bits)
    pieces = [add_up(p, "rows", row_bits[1:-1]) for p in pieces]
    others = [swap(p, "rows", row_bits[-1]) for p in pieces]
    data_next, beta_rows = data_out(data_total, data_sums, residuals)
    fresh, cell_squares = zip(
        *[fresh_piece(m, data_total, half, pieces[m], others[m], data_sums, cell_vec) for m in range(chunks)]
    )
    cell_sums = add_up(jnp.concatenate(cell_squares, 0), "cols", col_bits)
    cell_sums = add_up(cell_sums, "rows", row_bits[:1])
    gathered = [swap(f, "rows", row_bits[0]) for f in fresh]
    cell_next, alpha_rows = cell_out(cell_total, half, cell_sums, fresh, gathered)
    return (data_next, cell_next, spread_rows(beta_rows, part), spread_rows(alpha_rows, part))


def solution(mesh):
    placed = (
        P(("blocks", "rows"), "cols", None),
        P(("blocks", "rows"), "cols"),
        P(("blocks", "rows"), "cols"),
        P("blocks", "rows"),
        P("blocks", "cols"),
        P("blocks"),
    )
    return jax.shard_map(
        per_device,
        mesh=mesh,
        in_specs=placed,
        out_specs=(P("blocks", "rows"), P("blocks", "cols"), P("blocks"), P("blocks")),
        check_vma=False,
    )
```

time: 127 us -> 67.4 us (0.53)
  waiting for transfers between devices: 77 us -> 26.5 us
  starting transfers between devices: 0.08 us -> 25.1 us
  blocking collectives: 17.7 us -> 0 us
  between operations: 14.8 us -> 1.52 us
  other arithmetic: 9.5 us -> 0.2 us
  Pallas kernels: 0 us -> 9.06 us
  matrix products: 4.7 us -> 0 us
  local copies, waits for them, and re-layouts: 3.22 us -> 4.79 us
    psum x2 -> x0, waiting for transfers between devices: 76.9 us -> none  [the longest x1 41.3 us: per_device(): cell_full = lax.psum(partial_cells, 'rows')]
    ppermute x0 -> x25, waiting for transfers between devices: none -> 26.5 us  [swap(): lax.ppermute(value, axis, [(i, i ^ bit) for i in range(lax.axis_size(axis...]
    ppermute x0 -> x25, starting transfers between devices: none -> 25.1 us  [swap(): lax.ppermute(value, axis, [(i, i ^ bit) for i in range(lax.axis_size(axis...]
    psum x2 -> x0, blocking collectives: 17.7 us -> none  [the longest x1 11.7 us: per_device(): squares = lax.psum(jnp.sum(residual * residual, axis=1), 'rows')]
    pallas_call x0 -> x11, Pallas kernels: none -> 9.06 us  [the longest x4 4.88 us: backward(): pl.pallas_call(functools.partial(backward_kernel, m), out_shape=[piece, p...]
    dot_general x4 -> x0, matrix products: 4.7 us -> none  [the longest x1 1.71 us: adjoint_sweep(): jnp.einsum('ktj,ts->ksj', contrib, spread, precision=lax.Precision.HIGHEST)]
    convert_element_type x3 -> x0, other arithmetic: 3.06 us -> none  [the longest x1 1.88 us: per_device(): data_low = data_next.astype(jnp.bfloat16)]
    reduce_sum x2 -> x0, other arithmetic: 2.62 us -> none  [the longest x1 1.41 us: per_device(): sumsq = lax.psum(jnp.sum(fresh * fresh, axis=1), 'cols')]
  transfers between devices with their start and end apart: 2 -> 25, of which waited for: 2 -> 10; matrix products, arithmetic and copies ran while one was open for 0% -> 1% of each run, Pallas kernels for 0% -> 8%
where the time goes in v1:
time: 67.4 us; the launch traced here: 67.2 us
  waiting for transfers between devices  26.5 us (39%)
  starting transfers between devices  25.1 us (37%)
  Pallas kernels  9.06 us (13%)
  local copies, waits for them, and re-layouts  4.79 us (7%)
  between operations  1.52 us (2%)
    ppermute x25, waiting for transfers between devices, swap(): lax.ppermute(value, axis, [(i, i ^ bit) for i in range(lax.axis_size(axis...  26.5 us
    ppermute x25, starting transfers between devices, swap(): lax.ppermute(value, axis, [(i, i ^ bit) for i in range(lax.axis_size(axis...  25.1 us
    pallas_call x4, Pallas kernels, backward(): pl.pallas_call(functools.partial(backward_kernel, m), out_shape=[piece, p...  4.88 us
    unnamed x13, local copies, waits for them, and re-layouts  3.5 us
    pallas_call x1, Pallas kernels, forward(): pl.pallas_call(forward_kernel, out_shape=[jax.ShapeDtypeStruct((samples /...  1.49 us
  transfers between devices with their start and end apart: 25, of which 10 were waited for; matrix products, arithmetic and copies ran while one was open for 1% of the time, Pallas kernels for 8%

profile of v1, /device:TPU:0, one launch (start us, length us, event | category | flops | bytes accessed | tf_op | source)
XLA Modules:
  0.0 67.2 jit_solution(9445655717594823590)
XLA Ops:
  1.3 0.8 %copy.11.coords = s32[16,2]{1,0:T(8,128)S(1)} copy(s32[16,2]{0,1:T(2,128)} %param.7) | data formatting | bytes 256 | tf_op args[1]
  2.1 1.6 %copy-done = bf16[16,256,256]{2,1,0:T(8,128)(2,1)S(1)} copy-done((bf16[16,256,256]{2,1,0:T(8,128)(2,1)S(1)}, bf16[16,256,256]{2,1,0:T(8,128)(2,1)}, u32[]{:S(2)}) %copy-start) | copy-done | bytes 2097176
  3.7 1.1 %copy-done.2 = f32[96,2048]{1,0:T(8,128)S(1)} copy-done((f32[96,2048]{1,0:T(8,128)S(1)}, f32[96,2048]{1,0:T(8,128)}, u32[]{:S(2)}) %copy-start.2) | copy-done | bytes 786456
  4.8 1.5 %forward.1 = (f32[24,1024]{1,0:T(8,128)S(1)}, f32[24,1024]{1,0:T(8,128)S(1)}, f32[24,1024]{1,0:T(8,128)S(1)}, f32[24,1024]{1,0:T(8,128)S(1)}) custom-call(s32[16,2]{1,0:T(8,128)S(1)} %copy.11.coords, s32[1,1]{1,0:T(1,128)S(6)} %copy.19.count, f32[96,2048]{1,0:T(8,128)S(1)} %copy-done.2, bf16[16,256,256]{2,1,0:T(8,128)(2,1)S(1)} %copy-done), custom_call_target="tpu_custom_call" | custom-call | tf_op jit(solution)/shard_map/forward/pallas_call | solution.py:63
  6.3 3.0 %collective-permute-start = (f32[24,1024]{1,0:T(8,128)S(1)}, f32[24,1024]{1,0:T(8,128)S(1)}, u32[]{:S(2)}, u32[]{:S(2)}) collective-permute-start(f32[24,1024]{1,0:T(8,128)S(1)} %get-tuple-element.36), channel_id=1, source_target_pairs={{0,2},{1,3},{2,0},{3,1},{4,6},{5,7},{6,4},{7,5},{8,10},{9,11},{10,... | collective-permute-start | bytes 294920 | tf_op jit(solution)/shard_map/ppermute | solution.py:200
  9.3 0.1 collective-permute-start.2
  9.4 1.9 %collective-permute-start.4 = (f32[24,1024]{1,0:T(8,128)S(1)}, f32[24,1024]{1,0:T(8,128)S(1)}, u32[]{:S(2)}, u32[]{:S(2)}) collective-permute-start(f32[24,1024]{1,0:T(8,128)S(1)} %get-tuple-element.40), channel_id=1, source_target_pairs={{0,2},{1,3},{2,0},{3,1},{4,6},{5,7},{6,4},{7,5},{8,10},{9,11},{10,... | collective-permute-start | bytes 294920 | tf_op jit(solution)/shard_map/ppermute | solution.py:200
  11.4 0.1 collective-permute-start.6
  11.4 1.3 %collective-permute-done = f32[24,1024]{1,0:T(8,128)S(1)} collective-permute-done((f32[24,1024]{1,0:T(8,128)S(1)}, f32[24,1024]{1,0:T(8,128)S(1)}, u32[]{:S(2)}, u32[]{:S(2)}) %collective-permute-start) | collective-permute-done | bytes 98336 | tf_op jit(solution)/shard_map/ppermute | solution.py:200
  12.8 0.1 collective-permute-start.1
  12.9 2.1 %collective-permute-done.2 = f32[24,1024]{1,0:T(8,128)S(1)} collective-permute-done((f32[24,1024]{1,0:T(8,128)S(1)}, f32[24,1024]{1,0:T(8,128)S(1)}, u32[]{:S(2)}, u32[]{:S(2)}) %collective-permute-start.2) | collective-permute-done | bytes 98336 | tf_op jit(solution)/shard_map/ppermute | solution.py:200
  15.0 0.1 collective-permute-start.3
  15.1 2.0 %collective-permute-done.4 = f32[24,1024]{1,0:T(8,128)S(1)} collective-permute-done((f32[24,1024]{1,0:T(8,128)S(1)}, f32[24,1024]{1,0:T(8,128)S(1)}, u32[]{:S(2)}, u32[]{:S(2)}) %collective-permute-start.4) | collective-permute-done | bytes 98336 | tf_op jit(solution)/shard_map/ppermute | solution.py:200
  17.1 0.1 collective-permute-start.5
  17.2 1.2 %collective-permute-done.6 = f32[24,1024]{1,0:T(8,128)S(1)} collective-permute-done((f32[24,1024]{1,0:T(8,128)S(1)}, f32[24,1024]{1,0:T(8,128)S(1)}, u32[]{:S(2)}, u32[]{:S(2)}) %collective-permute-start.6) | collective-permute-done | bytes 98336 | tf_op jit(solution)/shard_map/ppermute | solution.py:200
  18.5 0.1 collective-permute-start.7
  18.6 0.1 copy.12.alpha_ref
  18.7 0.0 collective-permute-done.1.theirs
  18.7 1.2 %backward_0.1 = (f32[24,1024]{1,0:T(8,128)S(1)}, f32[24,1024]{1,0:T(8,128)S(1)}, f32[24,1024]{1,0:T(8,128)S(1)}, f32[1,128]{1,0:T(1,128)S(1)}) custom-call(s32[16,2]{1,0:T(8,128)S(1)} %copy.11.coords, s32[1,1]{1,0:T(1,128)S(6)} %copy.19.count, s32[1]{0:T(128)} %bitcast.half, f32[24,1024]{1,0:T(8,128)S(1)} %add.44.ours, ...), custom_call_target="tpu_custom_call" | custom-call | tf_op jit(solution)/shard_map/backward_0/pallas_call | solution.py:100
  19.9 0.0 collective-permute-done.3.theirs
  19.9 1.2 %backward_1.1 = (f32[24,1024]{1,0:T(8,128)S(1)}, f32[24,1024]{1,0:T(8,128)S(1)}, f32[24,1024]{1,0:T(8,128)S(1)}, f32[1,128]{1,0:T(1,128)S(1)}) custom-call(s32[16,2]{1,0:T(8,128)S(1)} %copy.11.coords, s32[1,1]{1,0:T(1,128)S(6)} %copy.19.count, s32[1]{0:T(128)} %bitcast.half, f32[24,1024]{1,0:T(8,128)S(1)} %add.45.ours, ...), custom_call_target="tpu_custom_call" | custom-call | tf_op jit(solution)/shard_map/backward_1/pallas_call | solution.py:100
  21.2 0.0 collective-permute-done.5.theirs
  21.2 1.2 %backward_2.1 = (f32[24,1024]{1,0:T(8,128)S(1)}, f32[24,1024]{1,0:T(8,128)S(1)}, f32[24,1024]{1,0:T(8,128)S(1)}, f32[1,128]{1,0:T(1,128)S(1)}) custom-call(s32[16,2]{1,0:T(8,128)S(1)} %copy.11.coords, s32[1,1]{1,0:T(1,128)S(6)} %copy.19.count, s32[1]{0:T(128)} %bitcast.half, f32[24,1024]{1,0:T(8,128)S(1)} %add.46.ours, ...), custom_call_target="tpu_custom_call" | custom-call | tf_op jit(solution)/shard_map/backward_2/pallas_call | solution.py:100
  22.4 0.0 copy-start.3
  22.4 0.0 collective-permute-done.7.theirs
  22.4 1.2 %backward_3.1 = (f32[24,1024]{1,0:T(8,128)S(1)}, f32[24,1024]{1,0:T(8,128)S(1)}, f32[24,1024]{1,0:T(8,128)S(1)}, f32[1,128]{1,0:T(1,128)S(1)}) custom-call(s32[16,2]{1,0:T(8,128)S(1)} %copy.11.coords, s32[1,1]{1,0:T(1,128)S(6)} %copy.19.count, s32[1]{0:T(128)} %bitcast.half, f32[24,1024]{1,0:T(8,128)S(1)} %add.47.ours, ...), custom_call_target="tpu_custom_call" | custom-call | tf_op jit(solution)/shard_map/backward_3/pallas_call | solution.py:100
  23.7 2.0 %collective-permute-start.8 = (f32[4,128]{1,0:T(4,128)S(1)}, f32[4,128]{1,0:T(4,128)S(1)}, u32[]{:S(2)}, u32[]{:S(2)}) collective-permute-start(f32[4,128]{1,0:T(4,128)S(1)} %pad_maximum_fusion), channel_id=1, source_target_pairs={{0,4},{4,0},{8,12},{12,8},{1,5},{5,1},{9,13},{13,9},{2,6},{6,2},{1... | collective-permute-start | bytes 6152 | tf_op jit(solution)/shard_map/ppermute | solution.py:200
  25.6 0.1 collective-permute-start.10
  25.7 1.9 %collective-permute-start.12 = (f32[24,1024]{1,0:T(8,128)S(1)}, f32[24,1024]{1,0:T(8,128)S(1)}, u32[]{:S(2)}, u32[]{:S(2)}) collective-permute-start(f32[24,1024]{1,0:T(8,128)S(1)} %get-tuple-element.53), channel_id=1, source_target_pairs={{0,4},{4,0},{8,12},{12,8},{1,5},{5,1},{9,13},{13,9},{2,6},{6,2},{1... | collective-permute-start | bytes 294920 | tf_op jit(solution)/shard_map/ppermute | solution.py:200
  27.6 0.1 collective-permute-start.14
  27.8 1.9 %collective-permute-start.16 = (f32[24,1024]{1,0:T(8,128)S(1)}, f32[24,1024]{1,0:T(8,128)S(1)}, u32[]{:S(2)}, u32[]{:S(2)}) collective-permute-start(f32[24,1024]{1,0:T(8,128)S(1)} %get-tuple-element.59), channel_id=1, source_target_pairs={{0,4},{4,0},{8,12},{12,8},{1,5},{5,1},{9,13},{13,9},{2,6},{6,2},{1... | collective-permute-start | bytes 294920 | tf_op jit(solution)/shard_map/ppermute | solution.py:200
  29.7 0.0 collective-permute-done.8
  29.7 2.7 %collective-permute-start.9 = (f32[4,128]{1,0:T(4,128)S(1)}, f32[4,128]{1,0:T(4,128)S(1)}, u32[]{:S(2)}, u32[]{:S(2)}) collective-permute-start(f32[4,128]{1,0:T(4,128)S(1)} %fusion.1), channel_id=1, source_target_pairs={{0,8},{4,12},{8,0},{12,4},{1,9},{5,13},{9,1},{13,5},{2,10},{6,14},... | collective-permute-start | bytes 6152 | tf_op jit(solution)/shard_map/ppermute | solution.py:200
  32.4 0.0 collective-permute-done.10
  32.4 1.6 %collective-permute-start.11 = (f32[24,1024]{1,0:T(8,128)S(1)}, f32[24,1024]{1,0:T(8,128)S(1)}, u32[]{:S(2)}, u32[]{:S(2)}) collective-permute-start(f32[24,1024]{1,0:T(8,128)S(1)} %add.50.ours), channel_id=1, source_target_pairs={{0,8},{4,12},{8,0},{12,4},{1,9},{5,13},{9,1},{13,5},{2,10},{6,14},... | collective-permute-start | bytes 294920 | tf_op jit(solution)/shard_map/ppermute | solution.py:200
  34.0 0.0 collective-permute-done.12
  34.0 2.1 %collective-permute-start.13 = (f32[24,1024]{1,0:T(8,128)S(1)}, f32[24,1024]{1,0:T(8,128)S(1)}, u32[]{:S(2)}, u32[]{:S(2)}) collective-permute-start(f32[24,1024]{1,0:T(8,128)S(1)} %add.51.ours), channel_id=1, source_target_pairs={{0,8},{4,12},{8,0},{12,4},{1,9},{5,13},{9,1},{13,5},{2,10},{6,14},... | collective-permute-start | bytes 294920 | tf_op jit(solution)/shard_map/ppermute | solution.py:200
  36.1 3.5 %collective-permute-done.14 = f32[24,1024]{1,0:T(8,128)S(1)} collective-permute-done((f32[24,1024]{1,0:T(8,128)S(1)}, f32[24,1024]{1,0:T(8,128)S(1)}, u32[]{:S(2)}, u32[]{:S(2)}) %collective-permute-start.14) | collective-permute-done | bytes 98336 | tf_op jit(solution)/shard_map/ppermute | solution.py:200
  39.6 0.1 collective-permute-start.15
  39.7 1.4 %collective-permute-done.16 = f32[24,1024]{1,0:T(8,128)S(1)} collective-permute-done((f32[24,1024]{1,0:T(8,128)S(1)}, f32[24,1024]{1,0:T(8,128)S(1)}, u32[]{:S(2)}, u32[]{:S(2)}) %collective-permute-start.16) | collective-permute-done | bytes 98336 | tf_op jit(solution)/shard_map/ppermute | solution.py:200
  41.1 1.6 %collective-permute-start.17 = (f32[24,1024]{1,0:T(8,128)S(1)}, f32[24,1024]{1,0:T(8,128)S(1)}, u32[]{:S(2)}, u32[]{:S(2)}) collective-permute-start(f32[24,1024]{1,0:T(8,128)S(1)} %add.53.ours), channel_id=1, source_target_pairs={{0,8},{4,12},{8,0},{12,4},{1,9},{5,13},{9,1},{13,5},{2,10},{6,14},... | collective-permute-start | bytes 294920 | tf_op jit(solution)/shard_map/ppermute | solution.py:200
  42.7 7.9 %collective-permute-done.15.theirs = f32[24,1024]{1,0:T(8,128)S(1)} collective-permute-done((f32[24,1024]{1,0:T(8,128)S(1)}, f32[24,1024]{1,0:T(8,128)S(1)}, u32[]{:S(2)}, u32[]{:S(2)}) %collective-permute-start.15) | collective-permute-done | bytes 98336 | tf_op jit(solution)/shard_map/ppermute | solution.py:200
  50.6 0.2 fresh_2.1
  50.8 0.0 collective-permute-done.13.theirs
  50.8 0.2 fresh_1.1
  51.0 0.2 fresh_0.1
  51.2 0.4 collective-permute-done.17.theirs
  51.7 0.2 fresh_3.1
  51.9 0.1 collective-permute-start.18
  52.0 1.1 %collective-permute-done.18 = f32[4,128]{1,0:T(4,128)S(1)} collective-permute-done((f32[4,128]{1,0:T(4,128)S(1)}, f32[4,128]{1,0:T(4,128)S(1)}, u32[]{:S(2)}, u32[]{:S(2)}) %collective-permute-start.18) | collective-permute-done | bytes 2080 | tf_op jit(solution)/shard_map/ppermute | solution.py:200
  53.1 1.5 %collective-permute-start.19 = (f32[4,128]{1,0:T(4,128)S(1)}, f32[4,128]{1,0:T(4,128)S(1)}, u32[]{:S(2)}, u32[]{:S(2)}) collective-permute-start(f32[4,128]{1,0:T(4,128)S(1)} %fusion), channel_id=1, source_target_pairs={{0,2},{1,3},{2,0},{3,1},{4,6},{5,7},{6,4},{7,5},{8,10},{9,11},{10,... | collective-permute-start | bytes 6152 | tf_op jit(solution)/shard_map/ppermute | solution.py:200
  54.6 0.0 collective-permute-start.23
  54.6 2.0 %collective-permute-start.22 = (f32[24,1024]{1,0:T(8,128)S(1)}, f32[24,1024]{1,0:T(8,128)S(1)}, u32[]{:S(2)}, u32[]{:S(2)}) collective-permute-start(f32[24,1024]{1,0:T(8,128)S(1)} %get-tuple-element.62.rest_1_), channel_id=1, source_target_pairs={{0,4},{4,0},{8,12},{12,8},{1,5},{5,1},{9,13},{13,9},{2,6},{6,2},{1... | collective-permute-start | bytes 294920 | tf_op jit(solution)/shard_map/ppermute | solution.py:200
  56.6 0.0 collective-permute-start.21
  56.7 2.0 %collective-permute-start.24 = (f32[24,1024]{1,0:T(8,128)S(1)}, f32[24,1024]{1,0:T(8,128)S(1)}, u32[]{:S(2)}, u32[]{:S(2)}) collective-permute-start(f32[24,1024]{1,0:T(8,128)S(1)} %get-tuple-element.64.rest_3_), channel_id=1, source_target_pairs={{0,4},{4,0},{8,12},{12,8},{1,5},{5,1},{9,13},{13,9},{2,6},{6,2},{1... | collective-permute-start | bytes 294920 | tf_op jit(solution)/shard_map/ppermute | solution.py:200
  58.7 0.1 collective-permute-start.20
  58.8 0.9 %data_out.1 = (f32[96,1024]{1,0:T(8,128)}, f32[4,128]{1,0:T(4,128)S(1)}) custom-call(f32[4,128]{1,0:T(4,128)S(1)} %fusion.3.sums, f32[24,1024]{1,0:T(8,128)S(1)} %get-tuple-element.44.rest_0_, f32[24,1024]{1,0:T(8,128)S(1)} %get-tuple-element.45.rest_1_, f32[24,1024]{1,0:T(8,128)S(1)} %get-tuple-element.46.rest_2_, f32[24,1024]{1,0:T(8,128)S(1)} %get-tuple-element.47.rest_3_), custom_call_target="tpu_custom_call" | custom-call | tf_op jit(solution)/shard_map/data_out/pallas_call | solution.py:151
  59.6 0.6 reshape.18
  60.2 5.3 %collective-permute-done.20 = f32[4,128]{1,0:T(4,128)S(1)} collective-permute-done((f32[4,128]{1,0:T(4,128)S(1)}, f32[4,128]{1,0:T(4,128)S(1)}, u32[]{:S(2)}, u32[]{:S(2)}) %collective-permute-start.20) | collective-permute-done | bytes 2080 | tf_op jit(solution)/shard_map/ppermute | solution.py:200
  65.6 0.0 collective-permute-done.23.rest_6_
  65.6 0.0 collective-permute-done.22.rest_5_
  65.6 0.0 collective-permute-done.24.rest_7_
  65.6 1.0 %cell_out.1 = (f32[96,2048]{1,0:T(8,128)}, f32[4,128]{1,0:T(4,128)S(1)}) custom-call(s32[1]{0:T(128)} %bitcast.half, f32[4,128]{1,0:T(4,128)S(1)} %add.56.sums, f32[24,1024]{1,0:T(8,128)S(1)} %get-tuple-element.61.rest_0_, f32[24,1024]{1,0:T(8,128)S(1)} %get-tuple-element.62.rest_1_, f32[24,1024]{1,0:T(8,128)S(1)} %get-tuple-element.63.rest_2_, ...), custom_call_target="tpu_custom_call" | custom-call | tf_op jit(solution)/shard_map/cell_out/pallas_call | solution.py:179
  66.6 0.6 reshape.19
  (28 shorter events, 0.2 us)
Async XLA Ops:
  0.6 17.9 %copy-start.5 = (f32[96]{0:T(128)S(1)}, f32[96]{0:T(128)}, u32[]{:S(2)}) copy-start(f32[96]{0:T(128)} %param.11) | copy-start | bytes 1156
  2.1 1.6 %copy-start = (bf16[16,256,256]{2,1,0:T(8,128)(2,1)S(1)}, bf16[16,256,256]{2,1,0:T(8,128)(2,1)}, u32[]{:S(2)}) copy-start(bf16[16,256,256]{2,1,0:T(8,128)(2,1)} %tiles_ref.9) | copy-start | bytes 6291460
  3.6 1.1 %copy-start.2 = (f32[96,2048]{1,0:T(8,128)S(1)}, f32[96,2048]{1,0:T(8,128)}, u32[]{:S(2)}) copy-start(f32[96,2048]{1,0:T(8,128)} %cell_ref.9) | copy-start | bytes 2359300
  4.8 13.9 %copy-start.1 = (bf16[16,256,256]{2,1,0:T(8,128)(2,1)S(1)}, bf16[16,256,256]{2,1,0:T(8,128)(2,1)}, u32[]{:S(2)}) copy-start(bf16[16,256,256]{2,1,0:T(8,128)(2,1)} %tiles_ref.9) | copy-start | bytes 6291460
  4.8 13.9 %copy-start.4 = (f32[96,1024]{1,0:T(8,128)S(1)}, f32[96,1024]{1,0:T(8,128)}, u32[]{:S(2)}) copy-start(f32[96,1024]{1,0:T(8,128)} %data_ref.7) | copy-start | bytes 1179652
  6.3 6.5 %collective-permute-start = (f32[24,1024]{1,0:T(8,128)S(1)}, f32[24,1024]{1,0:T(8,128)S(1)}, u32[]{:S(2)}, u32[]{:S(2)}) collective-permute-start(f32[24,1024]{1,0:T(8,128)S(1)} %get-tuple-element.36), channel_id=1, source_target_pairs={{0,2},{1,3},{2,0},{3,1},{4,6},{5,7},{6,4},{7,5},{8,10},{9,11},{10,... | collective-permute-start | bytes 294920 | tf_op jit(solution)/shard_map/ppermute | solution.py:200
  9.3 5.7 %collective-permute-start.2 = (f32[24,1024]{1,0:T(8,128)S(1)}, f32[24,1024]{1,0:T(8,128)S(1)}, u32[]{:S(2)}, u32[]{:S(2)}) collective-permute-start(f32[24,1024]{1,0:T(8,128)S(1)} %get-tuple-element.38), channel_id=1, source_target_pairs={{0,2},{1,3},{2,0},{3,1},{4,6},{5,7},{6,4},{7,5},{8,10},{9,11},{10,... | collective-permute-start | bytes 294920 | tf_op jit(solution)/shard_map/ppermute | solution.py:200
  9.4 7.7 %collective-permute-start.4 = (f32[24,1024]{1,0:T(8,128)S(1)}, f32[24,1024]{1,0:T(8,128)S(1)}, u32[]{:S(2)}, u32[]{:S(2)}) collective-permute-start(f32[24,1024]{1,0:T(8,128)S(1)} %get-tuple-element.40), channel_id=1, source_target_pairs={{0,2},{1,3},{2,0},{3,1},{4,6},{5,7},{6,4},{7,5},{8,10},{9,11},{10,... | collective-permute-start | bytes 294920 | tf_op jit(solution)/shard_map/ppermute | solution.py:200
  11.4 7.1 %collective-permute-start.6 = (f32[24,1024]{1,0:T(8,128)S(1)}, f32[24,1024]{1,0:T(8,128)S(1)}, u32[]{:S(2)}, u32[]{:S(2)}) collective-permute-start(f32[24,1024]{1,0:T(8,128)S(1)} %get-tuple-element.42), channel_id=1, source_target_pairs={{0,2},{1,3},{2,0},{3,1},{4,6},{5,7},{6,4},{7,5},{8,10},{9,11},{10,... | collective-permute-start | bytes 294920 | tf_op jit(solution)/shard_map/ppermute | solution.py:200
  12.8 5.9 %collective-permute-start.1 = (f32[24,1024]{1,0:T(8,128)S(1)}, f32[24,1024]{1,0:T(8,128)S(1)}, u32[]{:S(2)}, u32[]{:S(2)}) collective-permute-start(f32[24,1024]{1,0:T(8,128)S(1)} %add.44.ours), channel_id=1, source_target_pairs={{0,1},{1,0},{2,3},{3,2},{4,5},{5,4},{6,7},{7,6},{8,9},{9,8},{10,11... | collective-permute-start | bytes 294920 | tf_op jit(solution)/shard_map/ppermute | solution.py:200
  15.0 4.9 %collective-permute-start.3 = (f32[24,1024]{1,0:T(8,128)S(1)}, f32[24,1024]{1,0:T(8,128)S(1)}, u32[]{:S(2)}, u32[]{:S(2)}) collective-permute-start(f32[24,1024]{1,0:T(8,128)S(1)} %add.45.ours), channel_id=1, source_target_pairs={{0,1},{1,0},{2,3},{3,2},{4,5},{5,4},{6,7},{7,6},{8,9},{9,8},{10,11... | collective-permute-start | bytes 294920 | tf_op jit(solution)/shard_map/ppermute | solution.py:200
  17.1 4.0 %collective-permute-start.5 = (f32[24,1024]{1,0:T(8,128)S(1)}, f32[24,1024]{1,0:T(8,128)S(1)}, u32[]{:S(2)}, u32[]{:S(2)}) collective-permute-start(f32[24,1024]{1,0:T(8,128)S(1)} %add.46.ours), channel_id=1, source_target_pairs={{0,1},{1,0},{2,3},{3,2},{4,5},{5,4},{6,7},{7,6},{8,9},{9,8},{10,11... | collective-permute-start | bytes 294920 | tf_op jit(solution)/shard_map/ppermute | solution.py:200
  18.5 3.9 %collective-permute-start.7 = (f32[24,1024]{1,0:T(8,128)S(1)}, f32[24,1024]{1,0:T(8,128)S(1)}, u32[]{:S(2)}, u32[]{:S(2)}) collective-permute-start(f32[24,1024]{1,0:T(8,128)S(1)} %add.47.ours), channel_id=1, source_target_pairs={{0,1},{1,0},{2,3},{3,2},{4,5},{5,4},{6,7},{7,6},{8,9},{9,8},{10,11... | collective-permute-start | bytes 294920 | tf_op jit(solution)/shard_map/ppermute | solution.py:200
  22.4 28.2 %copy-start.3 = (f32[96,2048]{1,0:T(8,128)S(1)}, f32[96,2048]{1,0:T(8,128)}, u32[]{:S(2)}) copy-start(f32[96,2048]{1,0:T(8,128)} %cell_ref.9) | copy-start | bytes 2359300
  23.7 6.0 %collective-permute-start.8 = (f32[4,128]{1,0:T(4,128)S(1)}, f32[4,128]{1,0:T(4,128)S(1)}, u32[]{:S(2)}, u32[]{:S(2)}) collective-permute-start(f32[4,128]{1,0:T(4,128)S(1)} %pad_maximum_fusion), channel_id=1, source_target_pairs={{0,4},{4,0},{8,12},{12,8},{1,5},{5,1},{9,13},{13,9},{2,6},{6,2},{1... | collective-permute-start | bytes 6152 | tf_op jit(solution)/shard_map/ppermute | solution.py:200
  25.6 6.7 %collective-permute-start.10 = (f32[24,1024]{1,0:T(8,128)S(1)}, f32[24,1024]{1,0:T(8,128)S(1)}, u32[]{:S(2)}, u32[]{:S(2)}) collective-permute-start(f32[24,1024]{1,0:T(8,128)S(1)} %get-tuple-element.50), channel_id=1, source_target_pairs={{0,4},{4,0},{8,12},{12,8},{1,5},{5,1},{9,13},{13,9},{2,6},{6,2},{1... | collective-permute-start | bytes 294920 | tf_op jit(solution)/shard_map/ppermute | solution.py:200
  25.7 8.2 %collective-permute-start.12 = (f32[24,1024]{1,0:T(8,128)S(1)}, f32[24,1024]{1,0:T(8,128)S(1)}, u32[]{:S(2)}, u32[]{:S(2)}) collective-permute-start(f32[24,1024]{1,0:T(8,128)S(1)} %get-tuple-element.53), channel_id=1, source_target_pairs={{0,4},{4,0},{8,12},{12,8},{1,5},{5,1},{9,13},{13,9},{2,6},{6,2},{1... | collective-permute-start | bytes 294920 | tf_op jit(solution)/shard_map/ppermute | solution.py:200
  27.6 11.9 %collective-permute-start.14 = (f32[24,1024]{1,0:T(8,128)S(1)}, f32[24,1024]{1,0:T(8,128)S(1)}, u32[]{:S(2)}, u32[]{:S(2)}) collective-permute-start(f32[24,1024]{1,0:T(8,128)S(1)} %get-tuple-element.56), channel_id=1, source_target_pairs={{0,4},{4,0},{8,12},{12,8},{1,5},{5,1},{9,13},{13,9},{2,6},{6,2},{1... | collective-permute-start | bytes 294920 | tf_op jit(solution)/shard_map/ppermute | solution.py:200
  27.8 13.3 %collective-permute-start.16 = (f32[24,1024]{1,0:T(8,128)S(1)}, f32[24,1024]{1,0:T(8,128)S(1)}, u32[]{:S(2)}, u32[]{:S(2)}) collective-permute-start(f32[24,1024]{1,0:T(8,128)S(1)} %get-tuple-element.59), channel_id=1, source_target_pairs={{0,4},{4,0},{8,12},{12,8},{1,5},{5,1},{9,13},{13,9},{2,6},{6,2},{1... | collective-permute-start | bytes 294920 | tf_op jit(solution)/shard_map/ppermute | solution.py:200
  29.7 13.0 %collective-permute-start.9 = (f32[4,128]{1,0:T(4,128)S(1)}, f32[4,128]{1,0:T(4,128)S(1)}, u32[]{:S(2)}, u32[]{:S(2)}) collective-permute-start(f32[4,128]{1,0:T(4,128)S(1)} %fusion.1), channel_id=1, source_target_pairs={{0,8},{4,12},{8,0},{12,4},{1,9},{5,13},{9,1},{13,5},{2,10},{6,14},... | collective-permute-start | bytes 6152 | tf_op jit(solution)/shard_map/ppermute | solution.py:200
  32.4 18.7 %collective-permute-start.11 = (f32[24,1024]{1,0:T(8,128)S(1)}, f32[24,1024]{1,0:T(8,128)S(1)}, u32[]{:S(2)}, u32[]{:S(2)}) collective-permute-start(f32[24,1024]{1,0:T(8,128)S(1)} %add.50.ours), channel_id=1, source_target_pairs={{0,8},{4,12},{8,0},{12,4},{1,9},{5,13},{9,1},{13,5},{2,10},{6,14},... | collective-permute-start | bytes 294920 | tf_op jit(solution)/shard_map/ppermute | solution.py:200
  34.0 16.9 %collective-permute-start.13 = (f32[24,1024]{1,0:T(8,128)S(1)}, f32[24,1024]{1,0:T(8,128)S(1)}, u32[]{:S(2)}, u32[]{:S(2)}) collective-permute-start(f32[24,1024]{1,0:T(8,128)S(1)} %add.51.ours), channel_id=1, source_target_pairs={{0,8},{4,12},{8,0},{12,4},{1,9},{5,13},{9,1},{13,5},{2,10},{6,14},... | collective-permute-start | bytes 294920 | tf_op jit(solution)/shard_map/ppermute | solution.py:200
  39.6 11.0 %collective-permute-start.15 = (f32[24,1024]{1,0:T(8,128)S(1)}, f32[24,1024]{1,0:T(8,128)S(1)}, u32[]{:S(2)}, u32[]{:S(2)}) collective-permute-start(f32[24,1024]{1,0:T(8,128)S(1)} %add.52.ours), channel_id=1, source_target_pairs={{0,8},{4,12},{8,0},{12,4},{1,9},{5,13},{9,1},{13,5},{2,10},{6,14},... | collective-permute-start | bytes 294920 | tf_op jit(solution)/shard_map/ppermute | solution.py:200
  41.1 10.6 %collective-permute-start.17 = (f32[24,1024]{1,0:T(8,128)S(1)}, f32[24,1024]{1,0:T(8,128)S(1)}, u32[]{:S(2)}, u32[]{:S(2)}) collective-permute-start(f32[24,1024]{1,0:T(8,128)S(1)} %add.53.ours), channel_id=1, source_target_pairs={{0,8},{4,12},{8,0},{12,4},{1,9},{5,13},{9,1},{13,5},{2,10},{6,14},... | collective-permute-start | bytes 294920 | tf_op jit(solution)/shard_map/ppermute | solution.py:200
  51.9 1.2 %collective-permute-start.18 = (f32[4,128]{1,0:T(4,128)S(1)}, f32[4,128]{1,0:T(4,128)S(1)}, u32[]{:S(2)}, u32[]{:S(2)}) collective-permute-start(f32[4,128]{1,0:T(4,128)S(1)} %pad_maximum_fusion.1), channel_id=1, source_target_pairs={{0,1},{1,0},{2,3},{3,2},{4,5},{5,4},{6,7},{7,6},{8,9},{9,8},{10,11... | collective-permute-start | bytes 6152 | tf_op jit(solution)/shard_map/ppermute | solution.py:200
  53.1 5.5 %collective-permute-start.19 = (f32[4,128]{1,0:T(4,128)S(1)}, f32[4,128]{1,0:T(4,128)S(1)}, u32[]{:S(2)}, u32[]{:S(2)}) collective-permute-start(f32[4,128]{1,0:T(4,128)S(1)} %fusion), channel_id=1, source_target_pairs={{0,2},{1,3},{2,0},{3,1},{4,6},{5,7},{6,4},{7,5},{8,10},{9,11},{10,... | collective-permute-start | bytes 6152 | tf_op jit(solution)/shard_map/ppermute | solution.py:200
  54.6 11.0 %collective-permute-start.23 = (f32[24,1024]{1,0:T(8,128)S(1)}, f32[24,1024]{1,0:T(8,128)S(1)}, u32[]{:S(2)}, u32[]{:S(2)}) collective-permute-start(f32[24,1024]{1,0:T(8,128)S(1)} %get-tuple-element.63.rest_2_), channel_id=1, source_target_pairs={{0,4},{4,0},{8,12},{12,8},{1,5},{5,1},{9,13},{13,9},{2,6},{6,2},{1... | collective-permute-start | bytes 294920 | tf_op jit(solution)/shard_map/ppermute | solution.py:200
  54.6 11.0 %collective-permute-start.22 = (f32[24,1024]{1,0:T(8,128)S(1)}, f32[24,1024]{1,0:T(8,128)S(1)}, u32[]{:S(2)}, u32[]{:S(2)}) collective-permute-start(f32[24,1024]{1,0:T(8,128)S(1)} %get-tuple-element.62.rest_1_), channel_id=1, source_target_pairs={{0,4},{4,0},{8,12},{12,8},{1,5},{5,1},{9,13},{13,9},{2,6},{6,2},{1... | collective-permute-start | bytes 294920 | tf_op jit(solution)/shard_map/ppermute | solution.py:200
  56.6 8.9 %collective-permute-start.21 = (f32[24,1024]{1,0:T(8,128)S(1)}, f32[24,1024]{1,0:T(8,128)S(1)}, u32[]{:S(2)}, u32[]{:S(2)}) collective-permute-start(f32[24,1024]{1,0:T(8,128)S(1)} %get-tuple-element.61.rest_0_), channel_id=1, source_target_pairs={{0,4},{4,0},{8,12},{12,8},{1,5},{5,1},{9,13},{13,9},{2,6},{6,2},{1... | collective-permute-start | bytes 294920 | tf_op jit(solution)/shard_map/ppermute | solution.py:200
  56.7 8.9 %collective-permute-start.24 = (f32[24,1024]{1,0:T(8,128)S(1)}, f32[24,1024]{1,0:T(8,128)S(1)}, u32[]{:S(2)}, u32[]{:S(2)}) collective-permute-start(f32[24,1024]{1,0:T(8,128)S(1)} %get-tuple-element.64.rest_3_), channel_id=1, source_target_pairs={{0,4},{4,0},{8,12},{12,8},{1,5},{5,1},{9,13},{13,9},{2,6},{6,2},{1... | collective-permute-start | bytes 294920 | tf_op jit(solution)/shard_map/ppermute | solution.py:200
  58.7 6.9 %collective-permute-start.20 = (f32[4,128]{1,0:T(4,128)S(1)}, f32[4,128]{1,0:T(4,128)S(1)}, u32[]{:S(2)}, u32[]{:S(2)}) collective-permute-start(f32[4,128]{1,0:T(4,128)S(1)} %fusion.2), channel_id=1, source_target_pairs={{0,4},{4,0},{8,12},{12,8},{1,5},{5,1},{9,13},{13,9},{2,6},{6,2},{1... | collective-permute-start | bytes 6152 | tf_op jit(solution)/shard_map/ppermute | solution.py:200
